TPU v7x, 32 devices: a whole 2x2x4 slice. The times are simulated.
32 devices in a mesh: tile: 8 (over z, y), cplx: 4 (over x, core).
Axes of the slice: x: 2, y: 2, z: 4, core: 2. Of those that a mesh axis runs over, the one named last changes fastest.
Arguments:
- pair_tiles: bfloat16 [96, 128, 128, 128], P(('tile', 'cplx'))
- tile_map: int32 [96, 3], replicated, may hold values from -1 to 3, as said below
- lengths: int32 [4], replicated, may hold values from 256 to 512
- resolved: int32 [4, 512], replicated, may hold values 0 or 1
- ln_gain: float32 [128], replicated, may hold values from 0.1 to 1.9
- w_in: bfloat16 [128, 512], replicated, may hold values from -0.5 to 0.5
- w_out: bfloat16 [512, 128], replicated, may hold values from -0.25 to 0.25
- w_head: bfloat16 [128, 64], replicated
- head_bias: float32 [64], replicated, may hold values from -4 to 4
Outputs:
- error_map: float32 [4, 512, 512], P('cplx', 'tile')
- residue_error: float32 [4, 512], P('cplx', 'tile')
- tm_score: float32 [4], P('cplx')
Inputs may be any that keep to these rules, and one draw needn't show every extreme that they name: `tile_map`: row (t * 4 + c) * 3 + j is slot j of the device at tile index t and cplx index c and holds the complex, block row and block column of its tile, or -1 three times where the slot is empty. Each tile (k, r, q) with r and q below ceil(lengths[k] / 128) is held by exactly one slot and no other tile is held. Complex k is owned by cplx index k // 1; no two filled slots of one device have the same owner, and for fixed t and j the owners over the 4 cplx indices are all different.
All inputs are finite; a program needn't handle non-finite values.
Results may differ from a plain program's by a relative error of at most 0.0089.
Values sent between devices are 32-bit elements; how exact they have to be, the bound alone decides.
No kernel may reach another device: no remote copies, remote signals or barrier semaphores. Data moves between devices by JAX's collectives and lax.ppermute only.
A program may use at most 128 MiB of HBM per device.

v0:
```python
import jax
import jax.numpy as jnp
from jax import lax
from jax.sharding import PartitionSpec as P

EPS = 1e-05


def bin_centers(bin_count):
    bin_step = 31.0 / (bin_count - 2)
    return (jnp.arange(bin_count, dtype=jnp.float32) + 0.5) * bin_step


def d_zero(length):
    clipped = jnp.maximum(length, 19).astype(jnp.float32)
    return 1.24 * jnp.cbrt(clipped - 15.0) - 1.8


def pair_head(row_block, ln_gain, w_in, w_out, w_head, head_bias, centers, distance):
    values = row_block.astype(jnp.float32)
    row_mean = jnp.mean(values, axis=-1, keepdims=True)
    centred = values - row_mean
    variance = jnp.mean(centred * centred, axis=-1, keepdims=True)
    normed = (centred * lax.rsqrt(variance + EPS) * ln_gain).astype(jnp.bfloat16)
    hidden = jax.nn.relu(jnp.dot(normed, w_in, preferred_element_type=jnp.float32)).astype(
        jnp.bfloat16
    )
    updated = (values + jnp.dot(hidden, w_out, preferred_element_type=jnp.float32)).astype(
        jnp.bfloat16
    )
    logits = jnp.dot(updated, w_head, preferred_element_type=jnp.float32) + head_bias
    bin_probs = jax.nn.softmax(logits, axis=-1)
    expected = jnp.sum(bin_probs * centers, axis=-1)
    tm_term = jnp.sum(bin_probs / (1.0 + (centers / distance) ** 2), axis=-1)
    return (expected, tm_term)


def route_rows(
    error_src, rows_src, row_src, found_src, n_tile, parts_per, rows_each, tile_side, highest
):
    target_rows = jnp.arange(n_tile, dtype=jnp.int32)[:, None, None]
    part_index = jnp.arange(parts_per, dtype=jnp.int32)[None, None, :]
    routing = (
        (target_rows == row_src[None, :, None] * parts_per + part_index) & found_src[None, :, None]
    ).astype(jnp.float32)
    sender_count = error_src.shape[0]
    error_parts = error_src.reshape(sender_count, parts_per, rows_each, tile_side)
    row_parts = rows_src.reshape(sender_count, parts_per, rows_each)
    error_out = jnp.einsum("tcq,cqrj->tcrj", routing, error_parts, precision=highest)
    rows_out = jnp.einsum("tcq,cqr->tcr", routing, row_parts, precision=highest)
    return (error_out, rows_out)


def place_rows(
    error_back,
    rows_back,
    member_all,
    row_all,
    colblk_all,
    found_all,
    row_index,
    parts_per,
    cpx_dev,
    blocks,
    rows_each,
    tile_side,
    maxres,
    highest,
):
    mine_rows = found_all & (row_all == row_index // parts_per)
    member_hot = (
        (jnp.arange(cpx_dev, dtype=jnp.int32)[None, None, :] == member_all[..., None])
        & mine_rows[..., None]
    ).astype(jnp.float32)
    block_hot = (
        jnp.arange(blocks, dtype=jnp.int32)[None, None, :] == colblk_all[..., None]
    ).astype(jnp.float32)
    sources = member_all.shape[0] * member_all.shape[1]
    place_hot = (member_hot[..., :, None] * block_hot[..., None, :]).reshape(
        sources, cpx_dev, blocks
    )
    share_map = jnp.einsum(
        "smb,srj->mrbj",
        place_hot,
        error_back.reshape(sources, rows_each, tile_side),
        precision=highest,
    ).reshape(cpx_dev, rows_each, maxres)
    share_rows = jnp.einsum(
        "sm,sr->mr",
        member_hot.reshape(sources, cpx_dev),
        rows_back.reshape(sources, rows_each),
        precision=highest,
    )
    return (share_map, share_rows)


def shards(pair_tiles, tile_map, lengths, resolved, ln_gain, w_in, w_out, w_head, head_bias):
    highest = lax.Precision.HIGHEST
    n_tile = lax.axis_size("tile")
    n_cplx = lax.axis_size("cplx")
    row_index = lax.axis_index("tile")
    col_index = lax.axis_index("cplx")
    slot_count, tile_side, _, pair_width = pair_tiles.shape
    complexes, maxres = resolved.shape
    blocks = maxres // tile_side
    cpx_dev = complexes // n_cplx
    rows_each = maxres // n_tile
    parts_per = tile_side // rows_each
    centers = bin_centers(w_head.shape[1])
    positions = jnp.arange(maxres, dtype=jnp.int32)
    valid_mask = ((positions[None, :] < lengths[:, None]) & (resolved > 0)).astype(jnp.float32)
    valid_blocks = valid_mask.reshape(complexes, blocks, tile_side)
    layout = tile_map.reshape(n_tile, n_cplx, slot_count, 3)
    own_slots = layout[row_index, col_index]
    row_count = tile_side * tile_side
    block_rows = min(4096, row_count)
    error_tiles = []
    score_tiles = []
    owner_list = []
    for slot in range(slot_count):
        slot_meta = own_slots[slot]
        present = slot_meta[0] >= 0
        complex_id = jnp.maximum(slot_meta[0], 0)
        block_row = jnp.maximum(slot_meta[1], 0)
        block_col = jnp.maximum(slot_meta[2], 0)
        distance = d_zero(lengths[complex_id])

        def head_block(row_block, distance=distance):
            return pair_head(row_block, ln_gain, w_in, w_out, w_head, head_bias, centers, distance)

        expected, tm_term = lax.map(
            head_block, pair_tiles[slot].reshape(row_count // block_rows, block_rows, pair_width)
        )
        row_valid = valid_blocks[complex_id, block_row]
        col_valid = valid_blocks[complex_id, block_col]
        weight = jnp.where(present, row_valid[:, None] * col_valid[None, :], jnp.float32(0.0))
        error_tiles.append(weight * expected.reshape(tile_side, tile_side))
        score_tiles.append(weight * tm_term.reshape(tile_side, tile_side))
        owner_list.append(jnp.where(present, complex_id // cpx_dev, -1))
    owner_ids = jnp.stack(owner_list)
    select = (jnp.arange(n_cplx, dtype=jnp.int32)[:, None] == owner_ids[None, :]).astype(
        jnp.float32
    )
    error_send = jnp.einsum("os,sij->oij", select, jnp.stack(error_tiles), precision=highest)
    score_send = jnp.einsum("os,sij->oij", select, jnp.stack(score_tiles), precision=highest)
    error_in, score_in = (
        lax.all_to_all(error_send, "cplx", split_axis=0, concat_axis=0, tiled=True),
        lax.all_to_all(score_send, "cplx", split_axis=0, concat_axis=0, tiled=True),
    )
    rows_in = jnp.sum(score_in, axis=2)
    complex_all = layout[..., 0]
    owner_all = jnp.where(complex_all >= 0, complex_all // cpx_dev, -1)
    matched = owner_all == col_index
    matched_float = matched.astype(jnp.float32)
    slot_hot = matched_float[row_index]
    error_slots = jnp.einsum("sj,sab->jab", slot_hot, error_in, precision=highest)
    rows_slots = jnp.einsum("sj,sa->ja", slot_hot, rows_in, precision=highest)
    found_slot = jnp.any(matched, axis=1)

    def pick_slot(column):
        return jnp.sum(jnp.where(matched, layout[..., column], 0), axis=1)

    member_slot = pick_slot(0) - col_index * cpx_dev
    row_slot = pick_slot(1)
    colblk_slot = pick_slot(2)
    error_out, rows_out = route_rows(
        error_slots,
        rows_slots,
        row_slot[row_index],
        found_slot[row_index],
        n_tile,
        parts_per,
        rows_each,
        tile_side,
        highest,
    )
    error_back, rows_back = (
        lax.all_to_all(error_out, "tile", split_axis=0, concat_axis=0, tiled=True),
        lax.all_to_all(rows_out, "tile", split_axis=0, concat_axis=0, tiled=True),
    )
    share_map, share_rows = place_rows(
        error_back,
        rows_back,
        member_slot,
        row_slot,
        colblk_slot,
        found_slot,
        row_index,
        parts_per,
        cpx_dev,
        blocks,
        rows_each,
        tile_side,
        maxres,
        highest,
    )
    valid_rows = lax.dynamic_slice(
        valid_mask, (col_index * cpx_dev, row_index * rows_each), (cpx_dev, rows_each)
    )
    totals = lax.dynamic_slice_in_dim(jnp.sum(valid_mask, axis=1), col_index * cpx_dev, cpx_dev)
    denominator = jnp.maximum(valid_rows * totals[:, None], jnp.float32(1.0))
    residue_error = jnp.sum(share_map, axis=2) / denominator
    best_share = jnp.max(share_rows / denominator, axis=1)
    tm_score = lax.pmax(best_share, "tile")
    return (share_map, residue_error, tm_score)


def solution(mesh):
    placed = (P(("tile", "cplx"), None, None, None), P(), P(), P(), P(), P(), P(), P(), P())
    return jax.shard_map(
        shards,
        mesh=mesh,
        in_specs=placed,
        out_specs=(P("cplx", "tile", None), P("cplx", "tile"), P("cplx")),
        check_vma=False,
    )
```

profile of v0, /device:TPU:0, one launch (start us, length us, event | category | flops | bytes accessed | tf_op | source)
XLA Modules:
  0.0 221.4 jit_solution(597201668748234575)
XLA Ops:
  0.6 0.8 reshape.667
  1.4 0.7 constant_dynamic-slice_fusion.12
  6.2 8.9 %fusion.147 = (bf16[1,128,128,128]{3,2,1,0:T(8,128)(2,1)}, bf16[1,128,128,128]{3,2,1,0:T(8,128)(2,1)}, bf16[1,128,128,128]{3,2,1,0:T(8,128)(2,1)}) fusion(bf16[3,128,128,128]{3,2,1,0:T(8,128)(2,1)} %param.15), kind=kLoop, calls=%fused_computation.187 | loop fusion | bytes 25165824 | tf_op jit(solution)/shard_map/slice | solution.py:132
  15.1 0.6 fusion.149
  16.5 38.7 %while.44 = (s32[]{:T(128)}, f32[4,4096]{1,0:T(4,128)S(1)}, f32[4,4096]{1,0:T(4,128)S(1)}, bf16[4,4096,128]{2,1,0:T(8,128)(2,1)}, f32[128]{0:T(128)S(1)}, /*inde...) while((s32[]{:T(128)}, f32[4,4096]{1,0:T(4,128)S(1)}, ...), condition=%wide.region_23.24_spmd.clone.clone, body=%wide.region_16.23_spmd.clone.clone.sunk | while | flops 1155256576 | bytes 10046353 | solution.py:131
  16.5 1.6 convert_reduce_fusion.8
  18.1 2.3 %fusion.225 = f32[4096]{0:T(1024)S(1)} fusion(f32[4096]{0:T(1024)S(1)} %broadcast_multiply_fusion.8, bf16[4,4096,128]{2,1,0:T(8,128)(2,1)} %get-tuple-element.704, s32[]{:T(128)S(6)} %copy.88), kind=kLoop, calls=%fused_computation.68.clone.1 | loop fusion | flops 2093056 | bytes 1081348 | tf_op jit(solution)/shard_map/while/body/eval_jaxpr/reduce_sum | solution.py:23
  20.4 4.1 %fusion.226 = bf16[4096,128]{1,0:T(8,128)(2,1)S(1)} fusion(bf16[512,128]{1,0:T(8,128)(2,1)S(1)} %get-tuple-element.707, bf16[128,512]{1,0:T(8,128)(2,1)S(1)} %get-tuple-element.706, f32[128]{0:T(128)S(1)} %get-tuple-element.705, f32[4096]{0:T(1024)S(1)} %add_rsqrt_fusion.8, f32[4096]{0:T(1024)S(1)} %broadcast_multiply_fusion.8, ...), kind=kOutput, calls=%fused_computation.61.clone.1 | convolution fusion | flops 1082130432 | bytes 3442176 | tf_op jit(solution)/shard_map/while/body/eval_jaxpr/dot_general | solution.py:28
  26.3 1.6 convert_reduce_fusion.8
  27.8 2.3 %fusion.225 = f32[4096]{0:T(1024)S(1)} fusion(f32[4096]{0:T(1024)S(1)} %broadcast_multiply_fusion.8, bf16[4,4096,128]{2,1,0:T(8,128)(2,1)} %get-tuple-element.704, s32[]{:T(128)S(6)} %copy.88), kind=kLoop, calls=%fused_computation.68.clone.1 | loop fusion | flops 2093056 | bytes 1081348 | tf_op jit(solution)/shard_map/while/body/eval_jaxpr/reduce_sum | solution.py:23
  30.2 4.0 %fusion.226 = bf16[4096,128]{1,0:T(8,128)(2,1)S(1)} fusion(bf16[512,128]{1,0:T(8,128)(2,1)S(1)} %get-tuple-element.707, bf16[128,512]{1,0:T(8,128)(2,1)S(1)} %get-tuple-element.706, f32[128]{0:T(128)S(1)} %get-tuple-element.705, f32[4096]{0:T(1024)S(1)} %add_rsqrt_fusion.8, f32[4096]{0:T(1024)S(1)} %broadcast_multiply_fusion.8, ...), kind=kOutput, calls=%fused_computation.61.clone.1 | convolution fusion | flops 1082130432 | bytes 3442176 | tf_op jit(solution)/shard_map/while/body/eval_jaxpr/dot_general | solution.py:28
  35.9 1.6 convert_reduce_fusion.8
  37.5 2.3 %fusion.225 = f32[4096]{0:T(1024)S(1)} fusion(f32[4096]{0:T(1024)S(1)} %broadcast_multiply_fusion.8, bf16[4,4096,128]{2,1,0:T(8,128)(2,1)} %get-tuple-element.704, s32[]{:T(128)S(6)} %copy.88), kind=kLoop, calls=%fused_computation.68.clone.1 | loop fusion | flops 2093056 | bytes 1081348 | tf_op jit(solution)/shard_map/while/body/eval_jaxpr/reduce_sum | solution.py:23
  39.8 4.2 %fusion.226 = bf16[4096,128]{1,0:T(8,128)(2,1)S(1)} fusion(bf16[512,128]{1,0:T(8,128)(2,1)S(1)} %get-tuple-element.707, bf16[128,512]{1,0:T(8,128)(2,1)S(1)} %get-tuple-element.706, f32[128]{0:T(128)S(1)} %get-tuple-element.705, f32[4096]{0:T(1024)S(1)} %add_rsqrt_fusion.8, f32[4096]{0:T(1024)S(1)} %broadcast_multiply_fusion.8, ...), kind=kOutput, calls=%fused_computation.61.clone.1 | convolution fusion | flops 1082130432 | bytes 3442176 | tf_op jit(solution)/shard_map/while/body/eval_jaxpr/dot_general | solution.py:28
  45.6 1.6 convert_reduce_fusion.8
  47.2 2.3 %fusion.225 = f32[4096]{0:T(1024)S(1)} fusion(f32[4096]{0:T(1024)S(1)} %broadcast_multiply_fusion.8, bf16[4,4096,128]{2,1,0:T(8,128)(2,1)} %get-tuple-element.704, s32[]{:T(128)S(6)} %copy.88), kind=kLoop, calls=%fused_computation.68.clone.1 | loop fusion | flops 2093056 | bytes 1081348 | tf_op jit(solution)/shard_map/while/body/eval_jaxpr/reduce_sum | solution.py:23
  49.6 4.0 %fusion.226 = bf16[4096,128]{1,0:T(8,128)(2,1)S(1)} fusion(bf16[512,128]{1,0:T(8,128)(2,1)S(1)} %get-tuple-element.707, bf16[128,512]{1,0:T(8,128)(2,1)S(1)} %get-tuple-element.706, f32[128]{0:T(128)S(1)} %get-tuple-element.705, f32[4096]{0:T(1024)S(1)} %add_rsqrt_fusion.8, f32[4096]{0:T(1024)S(1)} %broadcast_multiply_fusion.8, ...), kind=kOutput, calls=%fused_computation.61.clone.1 | convolution fusion | flops 1082130432 | bytes 3442176 | tf_op jit(solution)/shard_map/while/body/eval_jaxpr/dot_general | solution.py:28
  60.1 39.0 %while.42 = (s32[]{:T(128)}, f32[4,4096]{1,0:T(4,128)S(1)}, f32[4,4096]{1,0:T(4,128)S(1)}, bf16[4,4096,128]{2,1,0:T(8,128)(2,1)}, f32[128]{0:T(128)S(1)}, /*inde...) while((s32[]{:T(128)}, f32[4,4096]{1,0:T(4,128)S(1)}, ...), condition=%wide.region_7.8_spmd.clone.clone, body=%wide.region_0.7_spmd.clone.clone.sunk | while | flops 1155256576 | bytes 10046353 | solution.py:131
  60.1 1.6 convert_reduce_fusion.6
  61.7 2.3 %fusion.203 = f32[4096]{0:T(1024)S(1)} fusion(f32[4096]{0:T(1024)S(1)} %broadcast_multiply_fusion.6, bf16[4,4096,128]{2,1,0:T(8,128)(2,1)} %get-tuple-element.740, s32[]{:T(128)S(6)} %copy.97), kind=kLoop, calls=%fused_computation.12.clone.1 | loop fusion | flops 2093056 | bytes 1081348 | tf_op jit(solution)/shard_map/while/body/eval_jaxpr/reduce_sum | solution.py:23
  64.0 4.1 %fusion.204 = bf16[4096,128]{1,0:T(8,128)(2,1)S(1)} fusion(bf16[512,128]{1,0:T(8,128)(2,1)S(1)} %get-tuple-element.743, bf16[128,512]{1,0:T(8,128)(2,1)S(1)} %get-tuple-element.742, f32[128]{0:T(128)S(1)} %get-tuple-element.741, f32[4096]{0:T(1024)S(1)} %add_rsqrt_fusion.6, f32[4096]{0:T(1024)S(1)} %broadcast_multiply_fusion.6, ...), kind=kOutput, calls=%fused_computation.5.clone.1 | convolution fusion | flops 1082130432 | bytes 3442176 | tf_op jit(solution)/shard_map/while/body/eval_jaxpr/dot_general | solution.py:28
  69.8 1.6 convert_reduce_fusion.6
  71.4 2.3 %fusion.203 = f32[4096]{0:T(1024)S(1)} fusion(f32[4096]{0:T(1024)S(1)} %broadcast_multiply_fusion.6, bf16[4,4096,128]{2,1,0:T(8,128)(2,1)} %get-tuple-element.740, s32[]{:T(128)S(6)} %copy.97), kind=kLoop, calls=%fused_computation.12.clone.1 | loop fusion | flops 2093056 | bytes 1081348 | tf_op jit(solution)/shard_map/while/body/eval_jaxpr/reduce_sum | solution.py:23
  73.7 4.1 %fusion.204 = bf16[4096,128]{1,0:T(8,128)(2,1)S(1)} fusion(bf16[512,128]{1,0:T(8,128)(2,1)S(1)} %get-tuple-element.743, bf16[128,512]{1,0:T(8,128)(2,1)S(1)} %get-tuple-element.742, f32[128]{0:T(128)S(1)} %get-tuple-element.741, f32[4096]{0:T(1024)S(1)} %add_rsqrt_fusion.6, f32[4096]{0:T(1024)S(1)} %broadcast_multiply_fusion.6, ...), kind=kOutput, calls=%fused_computation.5.clone.1 | convolution fusion | flops 1082130432 | bytes 3442176 | tf_op jit(solution)/shard_map/while/body/eval_jaxpr/dot_general | solution.py:28
  79.5 1.6 convert_reduce_fusion.6
  81.1 2.3 %fusion.203 = f32[4096]{0:T(1024)S(1)} fusion(f32[4096]{0:T(1024)S(1)} %broadcast_multiply_fusion.6, bf16[4,4096,128]{2,1,0:T(8,128)(2,1)} %get-tuple-element.740, s32[]{:T(128)S(6)} %copy.97), kind=kLoop, calls=%fused_computation.12.clone.1 | loop fusion | flops 2093056 | bytes 1081348 | tf_op jit(solution)/shard_map/while/body/eval_jaxpr/reduce_sum | solution.py:23
  83.4 4.2 %fusion.204 = bf16[4096,128]{1,0:T(8,128)(2,1)S(1)} fusion(bf16[512,128]{1,0:T(8,128)(2,1)S(1)} %get-tuple-element.743, bf16[128,512]{1,0:T(8,128)(2,1)S(1)} %get-tuple-element.742, f32[128]{0:T(128)S(1)} %get-tuple-element.741, f32[4096]{0:T(1024)S(1)} %add_rsqrt_fusion.6, f32[4096]{0:T(1024)S(1)} %broadcast_multiply_fusion.6, ...), kind=kOutput, calls=%fused_computation.5.clone.1 | convolution fusion | flops 1082130432 | bytes 3442176 | tf_op jit(solution)/shard_map/while/body/eval_jaxpr/dot_general | solution.py:28
  89.2 1.6 convert_reduce_fusion.6
  90.8 2.3 %fusion.203 = f32[4096]{0:T(1024)S(1)} fusion(f32[4096]{0:T(1024)S(1)} %broadcast_multiply_fusion.6, bf16[4,4096,128]{2,1,0:T(8,128)(2,1)} %get-tuple-element.740, s32[]{:T(128)S(6)} %copy.97), kind=kLoop, calls=%fused_computation.12.clone.1 | loop fusion | flops 2093056 | bytes 1081348 | tf_op jit(solution)/shard_map/while/body/eval_jaxpr/reduce_sum | solution.py:23
  93.2 4.2 %fusion.204 = bf16[4096,128]{1,0:T(8,128)(2,1)S(1)} fusion(bf16[512,128]{1,0:T(8,128)(2,1)S(1)} %get-tuple-element.743, bf16[128,512]{1,0:T(8,128)(2,1)S(1)} %get-tuple-element.742, f32[128]{0:T(128)S(1)} %get-tuple-element.741, f32[4096]{0:T(1024)S(1)} %add_rsqrt_fusion.6, f32[4096]{0:T(1024)S(1)} %broadcast_multiply_fusion.6, ...), kind=kOutput, calls=%fused_computation.5.clone.1 | convolution fusion | flops 1082130432 | bytes 3442176 | tf_op jit(solution)/shard_map/while/body/eval_jaxpr/dot_general | solution.py:28
  100.0 38.7 %while.43 = (s32[]{:T(128)}, f32[4,4096]{1,0:T(4,128)S(1)}, f32[4,4096]{1,0:T(4,128)S(1)}, bf16[4,4096,128]{2,1,0:T(8,128)(2,1)}, f32[128]{0:T(128)S(1)}, /*inde...) while((s32[]{:T(128)}, f32[4,4096]{1,0:T(4,128)S(1)}, ...), condition=%wide.region_15.16_spmd.clone.clone, body=%wide.region_8.15_spmd.clone.clone.sunk | while | flops 1155256576 | bytes 10046353 | solution.py:131
  100.0 1.6 convert_reduce_fusion.7
  101.6 2.3 %fusion.214 = f32[4096]{0:T(1024)S(1)} fusion(f32[4096]{0:T(1024)S(1)} %broadcast_multiply_fusion.7, bf16[4,4096,128]{2,1,0:T(8,128)(2,1)} %get-tuple-element.776, s32[]{:T(128)S(6)} %copy.106), kind=kLoop, calls=%fused_computation.40.clone.1 | loop fusion | flops 2093056 | bytes 1081348 | tf_op jit(solution)/shard_map/while/body/eval_jaxpr/reduce_sum | solution.py:23
  103.9 4.0 %fusion.215 = bf16[4096,128]{1,0:T(8,128)(2,1)S(1)} fusion(bf16[512,128]{1,0:T(8,128)(2,1)S(1)} %get-tuple-element.779, bf16[128,512]{1,0:T(8,128)(2,1)S(1)} %get-tuple-element.778, f32[128]{0:T(128)S(1)} %get-tuple-element.777, f32[4096]{0:T(1024)S(1)} %add_rsqrt_fusion.7, f32[4096]{0:T(1024)S(1)} %broadcast_multiply_fusion.7, ...), kind=kOutput, calls=%fused_computation.33.clone.1 | convolution fusion | flops 1082130432 | bytes 3442176 | tf_op jit(solution)/shard_map/while/body/eval_jaxpr/dot_general | solution.py:28
  109.6 1.6 convert_reduce_fusion.7
  111.2 2.3 %fusion.214 = f32[4096]{0:T(1024)S(1)} fusion(f32[4096]{0:T(1024)S(1)} %broadcast_multiply_fusion.7, bf16[4,4096,128]{2,1,0:T(8,128)(2,1)} %get-tuple-element.776, s32[]{:T(128)S(6)} %copy.106), kind=kLoop, calls=%fused_computation.40.clone.1 | loop fusion | flops 2093056 | bytes 1081348 | tf_op jit(solution)/shard_map/while/body/eval_jaxpr/reduce_sum | solution.py:23
  113.5 4.0 %fusion.215 = bf16[4096,128]{1,0:T(8,128)(2,1)S(1)} fusion(bf16[512,128]{1,0:T(8,128)(2,1)S(1)} %get-tuple-element.779, bf16[128,512]{1,0:T(8,128)(2,1)S(1)} %get-tuple-element.778, f32[128]{0:T(128)S(1)} %get-tuple-element.777, f32[4096]{0:T(1024)S(1)} %add_rsqrt_fusion.7, f32[4096]{0:T(1024)S(1)} %broadcast_multiply_fusion.7, ...), kind=kOutput, calls=%fused_computation.33.clone.1 | convolution fusion | flops 1082130432 | bytes 3442176 | tf_op jit(solution)/shard_map/while/body/eval_jaxpr/dot_general | solution.py:28
  119.2 1.6 convert_reduce_fusion.7
  120.8 2.3 %fusion.214 = f32[4096]{0:T(1024)S(1)} fusion(f32[4096]{0:T(1024)S(1)} %broadcast_multiply_fusion.7, bf16[4,4096,128]{2,1,0:T(8,128)(2,1)} %get-tuple-element.776, s32[]{:T(128)S(6)} %copy.106), kind=kLoop, calls=%fused_computation.40.clone.1 | loop fusion | flops 2093056 | bytes 1081348 | tf_op jit(solution)/shard_map/while/body/eval_jaxpr/reduce_sum | solution.py:23
  123.2 4.0 %fusion.215 = bf16[4096,128]{1,0:T(8,128)(2,1)S(1)} fusion(bf16[512,128]{1,0:T(8,128)(2,1)S(1)} %get-tuple-element.779, bf16[128,512]{1,0:T(8,128)(2,1)S(1)} %get-tuple-element.778, f32[128]{0:T(128)S(1)} %get-tuple-element.777, f32[4096]{0:T(1024)S(1)} %add_rsqrt_fusion.7, f32[4096]{0:T(1024)S(1)} %broadcast_multiply_fusion.7, ...), kind=kOutput, calls=%fused_computation.33.clone.1 | convolution fusion | flops 1082130432 | bytes 3442176 | tf_op jit(solution)/shard_map/while/body/eval_jaxpr/dot_general | solution.py:28
  128.8 1.6 convert_reduce_fusion.7
  130.4 2.3 %fusion.214 = f32[4096]{0:T(1024)S(1)} fusion(f32[4096]{0:T(1024)S(1)} %broadcast_multiply_fusion.7, bf16[4,4096,128]{2,1,0:T(8,128)(2,1)} %get-tuple-element.776, s32[]{:T(128)S(6)} %copy.106), kind=kLoop, calls=%fused_computation.40.clone.1 | loop fusion | flops 2093056 | bytes 1081348 | tf_op jit(solution)/shard_map/while/body/eval_jaxpr/reduce_sum | solution.py:23
  132.7 4.1 %fusion.215 = bf16[4096,128]{1,0:T(8,128)(2,1)S(1)} fusion(bf16[512,128]{1,0:T(8,128)(2,1)S(1)} %get-tuple-element.779, bf16[128,512]{1,0:T(8,128)(2,1)S(1)} %get-tuple-element.778, f32[128]{0:T(128)S(1)} %get-tuple-element.777, f32[4096]{0:T(1024)S(1)} %add_rsqrt_fusion.7, f32[4096]{0:T(1024)S(1)} %broadcast_multiply_fusion.7, ...), kind=kOutput, calls=%fused_computation.33.clone.1 | convolution fusion | flops 1082130432 | bytes 3442176 | tf_op jit(solution)/shard_map/while/body/eval_jaxpr/dot_general | solution.py:28
  140.1 0.7 copy.42
  140.8 4.2 %all-to-all-start = ((f32[4,128,128]{2,1,0:T(8,128)}), f32[4,128,128]{2,1,0:T(8,128)S(1)}, u32[]{:S(2)}, u32[]{:S(2)}) async-start(f32[4,128,128]{2,1,0:T(8,128)} %copy.42), calls=%async_computation | async-start | bytes 524288 | tf_op jit(solution)/shard_map/all_to_all | solution.py:147
  146.0 0.5 fusion.85
  146.5 0.7 copy.52
  147.4 3.6 %all-to-all-done = f32[4,128,128]{2,1,0:T(8,128)S(1)} async-done(((f32[4,128,128]{2,1,0:T(8,128)}), f32[4,128,128]{2,1,0:T(8,128)S(1)}, u32[]{:S(2)}, u32[]{:S(2)}) %all-to-all-start) | async-done | bytes 262176 | tf_op jit(solution)/shard_map/all_to_all | solution.py:147
  151.1 3.4 %all-to-all-start.2 = ((f32[4,128,128]{2,1,0:T(8,128)}), f32[4,128,128]{2,1,0:T(8,128)S(1)}, u32[]{:S(2)}, u32[]{:S(2)}) async-start(f32[4,128,128]{2,1,0:T(8,128)} %copy.52), calls=%async_computation.2 | async-start | bytes 524288 | tf_op jit(solution)/shard_map/all_to_all | solution.py:148
  155.0 5.4 %all-to-all-done.2 = f32[4,128,128]{2,1,0:T(8,128)S(1)} async-done(((f32[4,128,128]{2,1,0:T(8,128)}), f32[4,128,128]{2,1,0:T(8,128)S(1)}, u32[]{:S(2)}, u32[]{:S(2)}) %all-to-all-start.2) | async-done | bytes 262176 | tf_op jit(solution)/shard_map/all_to_all | solution.py:148
  161.2 0.7 reshape.699
  161.9 6.4 %all-to-all-start.3 = ((f32[8,1,192]{2,1,0:T(1,128)}), f32[8,1,192]{2,1,0:T(1,128)S(1)}, u32[]{:S(2)}, u32[]{:S(2)}) async-start(f32[8,1,192]{2,1,0:T(1,128)} %reshape.699), calls=%async_computation.3 | async-start | bytes 16384 | tf_op jit(solution)/shard_map/all_to_all | solution.py:179
  168.4 0.6 convolution_bitcast_fusion
  169.0 1.0 copy.47
  170.0 4.9 %all-to-all-done.3 = f32[8,1,192]{2,1,0:T(1,128)S(1)} async-done(((f32[8,1,192]{2,1,0:T(1,128)}), f32[8,1,192]{2,1,0:T(1,128)S(1)}, u32[]{:S(2)}, u32[]{:S(2)}) %all-to-all-start.3) | async-done | bytes 6176 | tf_op jit(solution)/shard_map/all_to_all | solution.py:179
  174.9 3.5 %all-to-all-start.1 = ((f32[8,3,64,128]{3,2,1,0:T(8,128)}), f32[8,3,64,128]{3,2,1,0:T(8,128)S(1)}, u32[]{:S(2)}, u32[]{:S(2)}) async-start(f32[8,3,64,128]{3,2,1,0:T(8,128)} %copy.47), calls=%async_computation.1 | async-start | bytes 1572864 | tf_op jit(solution)/shard_map/all_to_all | solution.py:178
  178.8 0.6 dynamic_slice.69
  179.9 0.7 reduce.12
  180.6 16.5 %all-to-all-done.1 = f32[8,3,64,128]{3,2,1,0:T(8,128)S(1)} async-done(((f32[8,3,64,128]{3,2,1,0:T(8,128)}), f32[8,3,64,128]{3,2,1,0:T(8,128)S(1)}, u32[]{:S(2)}, u32[]{:S(2)}) %all-to-all-start.1) | async-done | bytes 786464 | tf_op jit(solution)/shard_map/all_to_all | solution.py:178
  197.2 1.5 fusion.150
  198.6 0.7 reshape.673
  199.3 1.2 bitcast_divide_fusion
  200.6 0.8 fusion.78
  201.4 20.0 %pmax.7 = f32[1]{0:T(128)} all-reduce(f32[1]{0:T(128)} %bitcast.53), channel_id=1, replica_groups=mesh['tile'=8,'cplx'=4] {'tile'}, use_global_device_ids=true, to_apply=%region_32.33 | all-reduce | flops 1 | bytes 8 | tf_op jit(solution)/shard_map/pmax | solution.py:204
  (155 shorter events, 24.8 us)
Async XLA Ops:
  6.1 9.0 %copy-start.3 = (s32[4]{0:T(128)S(1)}, s32[4]{0:T(128)}, u32[]{:S(2)}) copy-start(s32[4]{0:T(128)} %param.17) | copy-start | bytes 52
  6.1 10.3 %copy-start = (bf16[128,64]{0,1:T(8,128)(2,1)S(1)}, bf16[128,64]{0,1:T(8,128)(2,1)}, u32[]{:S(2)}) copy-start(bf16[128,64]{0,1:T(8,128)(2,1)} %param.22) | copy-start | bytes 49156
  6.2 10.3 %copy-start.1 = (f32[64]{0:T(128)S(1)}, f32[64]{0:T(128)}, u32[]{:S(2)}) copy-start(f32[64]{0:T(128)} %param.23) | copy-start | bytes 772
  6.2 10.3 %copy-start.4 = (bf16[128,512]{1,0:T(8,128)(2,1)S(1)}, bf16[128,512]{1,0:T(8,128)(2,1)}, u32[]{:S(2)}) copy-start(bf16[128,512]{1,0:T(8,128)(2,1)} %param.20) | copy-start | bytes 393220
  6.2 10.3 %copy-start.5 = (bf16[512,128]{1,0:T(8,128)(2,1)S(1)}, bf16[512,128]{1,0:T(8,128)(2,1)}, u32[]{:S(2)}) copy-start(bf16[512,128]{1,0:T(8,128)(2,1)} %param.21) | copy-start | bytes 393220
  6.2 10.3 %copy-start.6 = (f32[128]{0:T(128)S(1)}, f32[128]{0:T(128)}, u32[]{:S(2)}) copy-start(f32[128]{0:T(128)} %param.19) | copy-start | bytes 1540
  16.5 38.8 %copy-start.2 = (s32[4,512]{1,0:T(4,128)S(1)}, s32[4,512]{1,0:T(4,128)}, u32[]{:S(2)}) copy-start(s32[4,512]{1,0:T(4,128)} %param.18) | copy-start | bytes 24580
  140.8 10.2 %all-to-all-start = ((f32[4,128,128]{2,1,0:T(8,128)}), f32[4,128,128]{2,1,0:T(8,128)S(1)}, u32[]{:S(2)}, u32[]{:S(2)}) async-start(f32[4,128,128]{2,1,0:T(8,128)} %copy.42), calls=%async_computation | async-start | bytes 524288 | tf_op jit(solution)/shard_map/all_to_all | solution.py:147
  151.1 9.4 %all-to-all-start.2 = ((f32[4,128,128]{2,1,0:T(8,128)}), f32[4,128,128]{2,1,0:T(8,128)S(1)}, u32[]{:S(2)}, u32[]{:S(2)}) async-start(f32[4,128,128]{2,1,0:T(8,128)} %copy.52), calls=%async_computation.2 | async-start | bytes 524288 | tf_op jit(solution)/shard_map/all_to_all | solution.py:148
  161.9 13.0 %all-to-all-start.3 = ((f32[8,1,192]{2,1,0:T(1,128)}), f32[8,1,192]{2,1,0:T(1,128)S(1)}, u32[]{:S(2)}, u32[]{:S(2)}) async-start(f32[8,1,192]{2,1,0:T(1,128)} %reshape.699), calls=%async_computation.3 | async-start | bytes 16384 | tf_op jit(solution)/shard_map/all_to_all | solution.py:179
  174.9 22.3 %all-to-all-start.1 = ((f32[8,3,64,128]{3,2,1,0:T(8,128)}), f32[8,3,64,128]{3,2,1,0:T(8,128)S(1)}, u32[]{:S(2)}, u32[]{:S(2)}) async-start(f32[8,3,64,128]{3,2,1,0:T(8,128)} %copy.47), calls=%async_computation.1 | async-start | bytes 1572864 | tf_op jit(solution)/shard_map/all_to_all | solution.py:178
where the time goes:
time: 223 us; the launch traced here: 221 us
  matrix products  59.7 us (27%)
  other arithmetic  57.5 us (26%)
  waiting for transfers between devices  30.4 us (14%)
  local copies, waits for them, and re-layouts  24.1 us (11%)
  blocking collectives  20 us (9%)
  starting transfers between devices  17.6 us (8%)
  between operations  10.8 us (5%)
    dot_general x12, matrix products, pair_head(): jnp.dot(hidden, w_out, preferred_element_type=jnp.float32)  48.9 us
    reduce_sum x12, other arithmetic, pair_head(): variance = jnp.mean(centred * centred, axis=-1, keepdims=True)  27.9 us
    pmax x1, blocking collectives, shards(): tm_score = lax.pmax(best_share, 'tile')  20 us
    reduce_sum x12, other arithmetic, pair_head(): row_mean = jnp.mean(values, axis=-1, keepdims=True)  18.9 us
    all_to_all x1, waiting for transfers between devices, shards(): lax.all_to_all(error_out, 'tile', split_axis=0, concat_axis=0, tiled=True)  16.5 us
    slice x1, local copies, waits for them, and re-layouts, shards(): pair_tiles[slot].reshape(row_count // block_rows, block_rows, pair_width)  8.89 us
    all_to_all x1, starting transfers between devices, shards(): lax.all_to_all(rows_out, 'tile', split_axis=0, concat_axis=0, tiled=True)  6.45 us
    dynamic_update_slice x24, local copies, waits for them, and re-layouts, shards(): lax.map(head_block, pair_tiles[slot].reshape(row_count // block_rows, blo...  5.96 us
  transfers between devices with their start and end apart: 4, of which 4 were waited for; matrix products, arithmetic and copies ran while one was open for 3% of the time, Pallas kernels for 0%

commit v1 on v0

--- a/solution.py
+++ b/solution.py
@@ -4,6 +4,22 @@
 from jax.sharding import PartitionSpec as P
 
 EPS = 1e-05
+
+
+def exchange_in_pairs(value, axis, split, join):
+    ways, here = (lax.axis_size(axis), lax.axis_index(axis))
+    width = value.shape[split] // ways
+    shape = list(value.shape)
+    shape[split] = width
+    height = shape[join]
+    shape[join] = height * ways
+    full = jnp.zeros(shape, value.dtype)
+    for mask in range(ways):
+        part = lax.dynamic_slice_in_dim(value, (here ^ mask) * width, width, axis=split)
+        if mask:
+            part = lax.ppermute(part, axis, [(d, d ^ mask) for d in range(ways)])
+        full = lax.dynamic_update_slice_in_dim(full, part, (here ^ mask) * height, axis=join)
+    return full
 
 
 def bin_centers(bin_count):
@@ -176,7 +192,7 @@
     )
     error_back, rows_back = (
         lax.all_to_all(error_out, "tile", split_axis=0, concat_axis=0, tiled=True),
-        lax.all_to_all(rows_out, "tile", split_axis=0, concat_axis=0, tiled=True),
+        exchange_in_pairs(rows_out, "tile", 0, 0),
     )
     share_map, share_rows = place_rows(
         error_back,

time: 223 us -> 214 us (0.960)
  waiting for transfers between devices: 30.4 us -> 10.9 us
  starting transfers between devices: 17.6 us -> 29.5 us
    all_to_all x1, waiting for transfers between devices: 16.5 us -> 0.01 us  [shards(): lax.all_to_all(error_out, 'tile', split_axis=0, concat_axis=0, tiled=True)]
    ppermute x0 -> x7, starting transfers between devices: none -> 15.4 us  [exchange_in_pairs(): part = lax.ppermute(part, axis, [(d, d ^ mask) for d in range(ways)])]
    all_to_all x1 -> x0, starting transfers between devices: 6.45 us -> none  [shards(): lax.all_to_all(rows_out, 'tile', split_axis=0, concat_axis=0, tiled=True)]
    all_to_all x1 -> x0, waiting for transfers between devices: 4.86 us -> none  [shards(): lax.all_to_all(rows_out, 'tile', split_axis=0, concat_axis=0, tiled=True)]
    ppermute x0 -> x7, waiting for transfers between devices: none -> 3.44 us  [exchange_in_pairs(): part = lax.ppermute(part, axis, [(d, d ^ mask) for d in range(ways)])]
    all_to_all x1, starting transfers between devices: 3.55 us -> 6.45 us  [shards(): lax.all_to_all(error_out, 'tile', split_axis=0, concat_axis=0, tiled=True)]
  transfers between devices with their start and end apart: 4 -> 10, of which waited for: 4 -> 4; matrix products, arithmetic and copies ran while one was open for 3% -> 3% of each run, Pallas kernels for 0% -> 0%
where the time goes in v1:
time: 214 us; the launch traced here: 212 us
  matrix products  59.7 us (28%)
  other arithmetic  56.8 us (27%)
  starting transfers between devices  29.5 us (14%)
  local copies, waits for them, and re-layouts  23.2 us (11%)
  blocking collectives  20.2 us (9%)
  waiting for transfers between devices  10.9 us (5%)
  between operations  10.8 us (5%)
    dot_general x12, matrix products, pair_head(): jnp.dot(hidden, w_out, preferred_element_type=jnp.float32)  48.9 us
    reduce_sum x12, other arithmetic, pair_head(): variance = jnp.mean(centred * centred, axis=-1, keepdims=True)  27.9 us
    pmax x1, blocking collectives, shards(): tm_score = lax.pmax(best_share, 'tile')  20.2 us
    reduce_sum x12, other arithmetic, pair_head(): row_mean = jnp.mean(values, axis=-1, keepdims=True)  18.9 us
    ppermute x7, starting transfers between devices, exchange_in_pairs(): part = lax.ppermute(part, axis, [(d, d ^ mask) for d in range(ways)])  15.4 us
    slice x1, local copies, waits for them, and re-layouts, shards(): pair_tiles[slot].reshape(row_count // block_rows, block_rows, pair_width)  8.89 us
    all_to_all x1, starting transfers between devices, shards(): lax.all_to_all(error_out, 'tile', split_axis=0, concat_axis=0, tiled=True)  6.45 us
    dynamic_update_slice x24, local copies, waits for them, and re-layouts, shards(): lax.map(head_block, pair_tiles[slot].reshape(row_count // block_rows, blo...  5.96 us
  transfers between devices with their start and end apart: 10, of which 4 were waited for; matrix products, arithmetic and copies ran while one was open for 3% of the time, Pallas kernels for 0%

profile of v1, /device:TPU:0, one launch (start us, length us, event | category | flops | bytes accessed | tf_op | source)
XLA Modules:
  0.0 212.4 jit_solution(5217784567056216195)
XLA Ops:
  0.6 0.8 reshape.675
  1.4 0.7 constant_dynamic-slice_fusion.20
  6.2 8.9 %fusion.155 = (bf16[1,128,128,128]{3,2,1,0:T(8,128)(2,1)}, bf16[1,128,128,128]{3,2,1,0:T(8,128)(2,1)}, bf16[1,128,128,128]{3,2,1,0:T(8,128)(2,1)}) fusion(bf16[3,128,128,128]{3,2,1,0:T(8,128)(2,1)} %param.15), kind=kLoop, calls=%fused_computation.202 | loop fusion | bytes 25165824 | tf_op jit(solution)/shard_map/slice | solution.py:148
  16.5 38.7 %while.44 = (s32[]{:T(128)}, f32[4,4096]{1,0:T(4,128)S(1)}, f32[4,4096]{1,0:T(4,128)S(1)}, bf16[4,4096,128]{2,1,0:T(8,128)(2,1)}, f32[128]{0:T(128)S(1)}, /*inde...) while((s32[]{:T(128)}, f32[4,4096]{1,0:T(4,128)S(1)}, ...), condition=%wide.region_23.24_spmd.clone.clone, body=%wide.region_16.23_spmd.clone.clone.sunk | while | flops 1155256576 | bytes 10046353 | solution.py:147
  16.5 1.6 convert_reduce_fusion.8
  18.1 2.3 %fusion.234 = f32[4096]{0:T(1024)S(1)} fusion(f32[4096]{0:T(1024)S(1)} %broadcast_multiply_fusion.8, bf16[4,4096,128]{2,1,0:T(8,128)(2,1)} %get-tuple-element.712, s32[]{:T(128)S(6)} %copy.83), kind=kLoop, calls=%fused_computation.68.clone.1 | loop fusion | flops 2093056 | bytes 1081348 | tf_op jit(solution)/shard_map/while/body/eval_jaxpr/reduce_sum | solution.py:39
  20.4 4.1 %fusion.235 = bf16[4096,128]{1,0:T(8,128)(2,1)S(1)} fusion(bf16[512,128]{1,0:T(8,128)(2,1)S(1)} %get-tuple-element.715, bf16[128,512]{1,0:T(8,128)(2,1)S(1)} %get-tuple-element.714, f32[128]{0:T(128)S(1)} %get-tuple-element.713, f32[4096]{0:T(1024)S(1)} %add_rsqrt_fusion.8, f32[4096]{0:T(1024)S(1)} %broadcast_multiply_fusion.8, ...), kind=kOutput, calls=%fused_computation.61.clone.1 | convolution fusion | flops 1082130432 | bytes 3442176 | tf_op jit(solution)/shard_map/while/body/eval_jaxpr/dot_general | solution.py:44
  26.3 1.6 convert_reduce_fusion.8
  27.8 2.3 %fusion.234 = f32[4096]{0:T(1024)S(1)} fusion(f32[4096]{0:T(1024)S(1)} %broadcast_multiply_fusion.8, bf16[4,4096,128]{2,1,0:T(8,128)(2,1)} %get-tuple-element.712, s32[]{:T(128)S(6)} %copy.83), kind=kLoop, calls=%fused_computation.68.clone.1 | loop fusion | flops 2093056 | bytes 1081348 | tf_op jit(solution)/shard_map/while/body/eval_jaxpr/reduce_sum | solution.py:39
  30.2 4.0 %fusion.235 = bf16[4096,128]{1,0:T(8,128)(2,1)S(1)} fusion(bf16[512,128]{1,0:T(8,128)(2,1)S(1)} %get-tuple-element.715, bf16[128,512]{1,0:T(8,128)(2,1)S(1)} %get-tuple-element.714, f32[128]{0:T(128)S(1)} %get-tuple-element.713, f32[4096]{0:T(1024)S(1)} %add_rsqrt_fusion.8, f32[4096]{0:T(1024)S(1)} %broadcast_multiply_fusion.8, ...), kind=kOutput, calls=%fused_computation.61.clone.1 | convolution fusion | flops 1082130432 | bytes 3442176 | tf_op jit(solution)/shard_map/while/body/eval_jaxpr/dot_general | solution.py:44
  35.9 1.6 convert_reduce_fusion.8
  37.5 2.3 %fusion.234 = f32[4096]{0:T(1024)S(1)} fusion(f32[4096]{0:T(1024)S(1)} %broadcast_multiply_fusion.8, bf16[4,4096,128]{2,1,0:T(8,128)(2,1)} %get-tuple-element.712, s32[]{:T(128)S(6)} %copy.83), kind=kLoop, calls=%fused_computation.68.clone.1 | loop fusion | flops 2093056 | bytes 1081348 | tf_op jit(solution)/shard_map/while/body/eval_jaxpr/reduce_sum | solution.py:39
  39.8 4.2 %fusion.235 = bf16[4096,128]{1,0:T(8,128)(2,1)S(1)} fusion(bf16[512,128]{1,0:T(8,128)(2,1)S(1)} %get-tuple-element.715, bf16[128,512]{1,0:T(8,128)(2,1)S(1)} %get-tuple-element.714, f32[128]{0:T(128)S(1)} %get-tuple-element.713, f32[4096]{0:T(1024)S(1)} %add_rsqrt_fusion.8, f32[4096]{0:T(1024)S(1)} %broadcast_multiply_fusion.8, ...), kind=kOutput, calls=%fused_computation.61.clone.1 | convolution fusion | flops 1082130432 | bytes 3442176 | tf_op jit(solution)/shard_map/while/body/eval_jaxpr/dot_general | solution.py:44
  45.6 1.6 convert_reduce_fusion.8
  47.2 2.3 %fusion.234 = f32[4096]{0:T(1024)S(1)} fusion(f32[4096]{0:T(1024)S(1)} %broadcast_multiply_fusion.8, bf16[4,4096,128]{2,1,0:T(8,128)(2,1)} %get-tuple-element.712, s32[]{:T(128)S(6)} %copy.83), kind=kLoop, calls=%fused_computation.68.clone.1 | loop fusion | flops 2093056 | bytes 1081348 | tf_op jit(solution)/shard_map/while/body/eval_jaxpr/reduce_sum | solution.py:39
  49.6 4.0 %fusion.235 = bf16[4096,128]{1,0:T(8,128)(2,1)S(1)} fusion(bf16[512,128]{1,0:T(8,128)(2,1)S(1)} %get-tuple-element.715, bf16[128,512]{1,0:T(8,128)(2,1)S(1)} %get-tuple-element.714, f32[128]{0:T(128)S(1)} %get-tuple-element.713, f32[4096]{0:T(1024)S(1)} %add_rsqrt_fusion.8, f32[4096]{0:T(1024)S(1)} %broadcast_multiply_fusion.8, ...), kind=kOutput, calls=%fused_computation.61.clone.1 | convolution fusion | flops 1082130432 | bytes 3442176 | tf_op jit(solution)/shard_map/while/body/eval_jaxpr/dot_general | solution.py:44
  60.1 39.0 %while.42 = (s32[]{:T(128)}, f32[4,4096]{1,0:T(4,128)S(1)}, f32[4,4096]{1,0:T(4,128)S(1)}, bf16[4,4096,128]{2,1,0:T(8,128)(2,1)}, f32[128]{0:T(128)S(1)}, /*inde...) while((s32[]{:T(128)}, f32[4,4096]{1,0:T(4,128)S(1)}, ...), condition=%wide.region_7.8_spmd.clone.clone, body=%wide.region_0.7_spmd.clone.clone.sunk | while | flops 1155256576 | bytes 10046353 | solution.py:147
  60.1 1.6 convert_reduce_fusion.6
  61.7 2.3 %fusion.212 = f32[4096]{0:T(1024)S(1)} fusion(f32[4096]{0:T(1024)S(1)} %broadcast_multiply_fusion.6, bf16[4,4096,128]{2,1,0:T(8,128)(2,1)} %get-tuple-element.748, s32[]{:T(128)S(6)} %copy.92), kind=kLoop, calls=%fused_computation.12.clone.1 | loop fusion | flops 2093056 | bytes 1081348 | tf_op jit(solution)/shard_map/while/body/eval_jaxpr/reduce_sum | solution.py:39
  64.0 4.1 %fusion.213 = bf16[4096,128]{1,0:T(8,128)(2,1)S(1)} fusion(bf16[512,128]{1,0:T(8,128)(2,1)S(1)} %get-tuple-element.751, bf16[128,512]{1,0:T(8,128)(2,1)S(1)} %get-tuple-element.750, f32[128]{0:T(128)S(1)} %get-tuple-element.749, f32[4096]{0:T(1024)S(1)} %add_rsqrt_fusion.6, f32[4096]{0:T(1024)S(1)} %broadcast_multiply_fusion.6, ...), kind=kOutput, calls=%fused_computation.5.clone.1 | convolution fusion | flops 1082130432 | bytes 3442176 | tf_op jit(solution)/shard_map/while/body/eval_jaxpr/dot_general | solution.py:44
  69.8 1.6 convert_reduce_fusion.6
  71.4 2.3 %fusion.212 = f32[4096]{0:T(1024)S(1)} fusion(f32[4096]{0:T(1024)S(1)} %broadcast_multiply_fusion.6, bf16[4,4096,128]{2,1,0:T(8,128)(2,1)} %get-tuple-element.748, s32[]{:T(128)S(6)} %copy.92), kind=kLoop, calls=%fused_computation.12.clone.1 | loop fusion | flops 2093056 | bytes 1081348 | tf_op jit(solution)/shard_map/while/body/eval_jaxpr/reduce_sum | solution.py:39
  73.7 4.1 %fusion.213 = bf16[4096,128]{1,0:T(8,128)(2,1)S(1)} fusion(bf16[512,128]{1,0:T(8,128)(2,1)S(1)} %get-tuple-element.751, bf16[128,512]{1,0:T(8,128)(2,1)S(1)} %get-tuple-element.750, f32[128]{0:T(128)S(1)} %get-tuple-element.749, f32[4096]{0:T(1024)S(1)} %add_rsqrt_fusion.6, f32[4096]{0:T(1024)S(1)} %broadcast_multiply_fusion.6, ...), kind=kOutput, calls=%fused_computation.5.clone.1 | convolution fusion | flops 1082130432 | bytes 3442176 | tf_op jit(solution)/shard_map/while/body/eval_jaxpr/dot_general | solution.py:44
  79.5 1.6 convert_reduce_fusion.6
  81.1 2.3 %fusion.212 = f32[4096]{0:T(1024)S(1)} fusion(f32[4096]{0:T(1024)S(1)} %broadcast_multiply_fusion.6, bf16[4,4096,128]{2,1,0:T(8,128)(2,1)} %get-tuple-element.748, s32[]{:T(128)S(6)} %copy.92), kind=kLoop, calls=%fused_computation.12.clone.1 | loop fusion | flops 2093056 | bytes 1081348 | tf_op jit(solution)/shard_map/while/body/eval_jaxpr/reduce_sum | solution.py:39
  83.4 4.2 %fusion.213 = bf16[4096,128]{1,0:T(8,128)(2,1)S(1)} fusion(bf16[512,128]{1,0:T(8,128)(2,1)S(1)} %get-tuple-element.751, bf16[128,512]{1,0:T(8,128)(2,1)S(1)} %get-tuple-element.750, f32[128]{0:T(128)S(1)} %get-tuple-element.749, f32[4096]{0:T(1024)S(1)} %add_rsqrt_fusion.6, f32[4096]{0:T(1024)S(1)} %broadcast_multiply_fusion.6, ...), kind=kOutput, calls=%fused_computation.5.clone.1 | convolution fusion | flops 1082130432 | bytes 3442176 | tf_op jit(solution)/shard_map/while/body/eval_jaxpr/dot_general | solution.py:44
  89.2 1.6 convert_reduce_fusion.6
  90.8 2.3 %fusion.212 = f32[4096]{0:T(1024)S(1)} fusion(f32[4096]{0:T(1024)S(1)} %broadcast_multiply_fusion.6, bf16[4,4096,128]{2,1,0:T(8,128)(2,1)} %get-tuple-element.748, s32[]{:T(128)S(6)} %copy.92), kind=kLoop, calls=%fused_computation.12.clone.1 | loop fusion | flops 2093056 | bytes 1081348 | tf_op jit(solution)/shard_map/while/body/eval_jaxpr/reduce_sum | solution.py:39
  93.2 4.2 %fusion.213 = bf16[4096,128]{1,0:T(8,128)(2,1)S(1)} fusion(bf16[512,128]{1,0:T(8,128)(2,1)S(1)} %get-tuple-element.751, bf16[128,512]{1,0:T(8,128)(2,1)S(1)} %get-tuple-element.750, f32[128]{0:T(128)S(1)} %get-tuple-element.749, f32[4096]{0:T(1024)S(1)} %add_rsqrt_fusion.6, f32[4096]{0:T(1024)S(1)} %broadcast_multiply_fusion.6, ...), kind=kOutput, calls=%fused_computation.5.clone.1 | convolution fusion | flops 1082130432 | bytes 3442176 | tf_op jit(solution)/shard_map/while/body/eval_jaxpr/dot_general | solution.py:44
  100.0 38.7 %while.43 = (s32[]{:T(128)}, f32[4,4096]{1,0:T(4,128)S(1)}, f32[4,4096]{1,0:T(4,128)S(1)}, bf16[4,4096,128]{2,1,0:T(8,128)(2,1)}, f32[128]{0:T(128)S(1)}, /*inde...) while((s32[]{:T(128)}, f32[4,4096]{1,0:T(4,128)S(1)}, ...), condition=%wide.region_15.16_spmd.clone.clone, body=%wide.region_8.15_spmd.clone.clone.sunk | while | flops 1155256576 | bytes 10046353 | solution.py:147
  100.0 1.6 convert_reduce_fusion.7
  101.6 2.3 %fusion.223 = f32[4096]{0:T(1024)S(1)} fusion(f32[4096]{0:T(1024)S(1)} %broadcast_multiply_fusion.7, bf16[4,4096,128]{2,1,0:T(8,128)(2,1)} %get-tuple-element.784, s32[]{:T(128)S(6)} %copy.101), kind=kLoop, calls=%fused_computation.40.clone.1 | loop fusion | flops 2093056 | bytes 1081348 | tf_op jit(solution)/shard_map/while/body/eval_jaxpr/reduce_sum | solution.py:39
  103.9 4.0 %fusion.224 = bf16[4096,128]{1,0:T(8,128)(2,1)S(1)} fusion(bf16[512,128]{1,0:T(8,128)(2,1)S(1)} %get-tuple-element.787, bf16[128,512]{1,0:T(8,128)(2,1)S(1)} %get-tuple-element.786, f32[128]{0:T(128)S(1)} %get-tuple-element.785, f32[4096]{0:T(1024)S(1)} %add_rsqrt_fusion.7, f32[4096]{0:T(1024)S(1)} %broadcast_multiply_fusion.7, ...), kind=kOutput, calls=%fused_computation.33.clone.1 | convolution fusion | flops 1082130432 | bytes 3442176 | tf_op jit(solution)/shard_map/while/body/eval_jaxpr/dot_general | solution.py:44
  109.6 1.6 convert_reduce_fusion.7
  111.2 2.3 %fusion.223 = f32[4096]{0:T(1024)S(1)} fusion(f32[4096]{0:T(1024)S(1)} %broadcast_multiply_fusion.7, bf16[4,4096,128]{2,1,0:T(8,128)(2,1)} %get-tuple-element.784, s32[]{:T(128)S(6)} %copy.101), kind=kLoop, calls=%fused_computation.40.clone.1 | loop fusion | flops 2093056 | bytes 1081348 | tf_op jit(solution)/shard_map/while/body/eval_jaxpr/reduce_sum | solution.py:39
  113.5 4.0 %fusion.224 = bf16[4096,128]{1,0:T(8,128)(2,1)S(1)} fusion(bf16[512,128]{1,0:T(8,128)(2,1)S(1)} %get-tuple-element.787, bf16[128,512]{1,0:T(8,128)(2,1)S(1)} %get-tuple-element.786, f32[128]{0:T(128)S(1)} %get-tuple-element.785, f32[4096]{0:T(1024)S(1)} %add_rsqrt_fusion.7, f32[4096]{0:T(1024)S(1)} %broadcast_multiply_fusion.7, ...), kind=kOutput, calls=%fused_computation.33.clone.1 | convolution fusion | flops 1082130432 | bytes 3442176 | tf_op jit(solution)/shard_map/while/body/eval_jaxpr/dot_general | solution.py:44
  119.2 1.6 convert_reduce_fusion.7
  120.8 2.3 %fusion.223 = f32[4096]{0:T(1024)S(1)} fusion(f32[4096]{0:T(1024)S(1)} %broadcast_multiply_fusion.7, bf16[4,4096,128]{2,1,0:T(8,128)(2,1)} %get-tuple-element.784, s32[]{:T(128)S(6)} %copy.101), kind=kLoop, calls=%fused_computation.40.clone.1 | loop fusion | flops 2093056 | bytes 1081348 | tf_op jit(solution)/shard_map/while/body/eval_jaxpr/reduce_sum | solution.py:39
  123.2 4.0 %fusion.224 = bf16[4096,128]{1,0:T(8,128)(2,1)S(1)} fusion(bf16[512,128]{1,0:T(8,128)(2,1)S(1)} %get-tuple-element.787, bf16[128,512]{1,0:T(8,128)(2,1)S(1)} %get-tuple-element.786, f32[128]{0:T(128)S(1)} %get-tuple-element.785, f32[4096]{0:T(1024)S(1)} %add_rsqrt_fusion.7, f32[4096]{0:T(1024)S(1)} %broadcast_multiply_fusion.7, ...), kind=kOutput, calls=%fused_computation.33.clone.1 | convolution fusion | flops 1082130432 | bytes 3442176 | tf_op jit(solution)/shard_map/while/body/eval_jaxpr/dot_general | solution.py:44
  128.8 1.6 convert_reduce_fusion.7
  130.4 2.3 %fusion.223 = f32[4096]{0:T(1024)S(1)} fusion(f32[4096]{0:T(1024)S(1)} %broadcast_multiply_fusion.7, bf16[4,4096,128]{2,1,0:T(8,128)(2,1)} %get-tuple-element.784, s32[]{:T(128)S(6)} %copy.101), kind=kLoop, calls=%fused_computation.40.clone.1 | loop fusion | flops 2093056 | bytes 1081348 | tf_op jit(solution)/shard_map/while/body/eval_jaxpr/reduce_sum | solution.py:39
  132.7 4.1 %fusion.224 = bf16[4096,128]{1,0:T(8,128)(2,1)S(1)} fusion(bf16[512,128]{1,0:T(8,128)(2,1)S(1)} %get-tuple-element.787, bf16[128,512]{1,0:T(8,128)(2,1)S(1)} %get-tuple-element.786, f32[128]{0:T(128)S(1)} %get-tuple-element.785, f32[4096]{0:T(1024)S(1)} %add_rsqrt_fusion.7, f32[4096]{0:T(1024)S(1)} %broadcast_multiply_fusion.7, ...), kind=kOutput, calls=%fused_computation.33.clone.1 | convolution fusion | flops 1082130432 | bytes 3442176 | tf_op jit(solution)/shard_map/while/body/eval_jaxpr/dot_general | solution.py:44
  140.1 0.7 copy.41
  140.8 4.2 %all-to-all-start = ((f32[4,128,128]{2,1,0:T(8,128)}), f32[4,128,128]{2,1,0:T(8,128)S(1)}, u32[]{:S(2)}, u32[]{:S(2)}) async-start(f32[4,128,128]{2,1,0:T(8,128)} %copy.41), calls=%async_computation | async-start | bytes 524288 | tf_op jit(solution)/shard_map/all_to_all | solution.py:163
  146.5 0.7 copy.51
  147.3 3.7 %all-to-all-done = f32[4,128,128]{2,1,0:T(8,128)S(1)} async-done(((f32[4,128,128]{2,1,0:T(8,128)}), f32[4,128,128]{2,1,0:T(8,128)S(1)}, u32[]{:S(2)}, u32[]{:S(2)}) %all-to-all-start) | async-done | bytes 262176 | tf_op jit(solution)/shard_map/all_to_all | solution.py:163
  151.1 3.4 %all-to-all-start.2 = ((f32[4,128,128]{2,1,0:T(8,128)}), f32[4,128,128]{2,1,0:T(8,128)S(1)}, u32[]{:S(2)}, u32[]{:S(2)}) async-start(f32[4,128,128]{2,1,0:T(8,128)} %copy.51), calls=%async_computation.2 | async-start | bytes 524288 | tf_op jit(solution)/shard_map/all_to_all | solution.py:164
  155.0 0.6 convolution_bitcast_fusion
  155.6 1.0 copy.46
  156.7 3.8 %all-to-all-done.2 = f32[4,128,128]{2,1,0:T(8,128)S(1)} async-done(((f32[4,128,128]{2,1,0:T(8,128)}), f32[4,128,128]{2,1,0:T(8,128)S(1)}, u32[]{:S(2)}, u32[]{:S(2)}) %all-to-all-start.2) | async-done | bytes 262176 | tf_op jit(solution)/shard_map/all_to_all | solution.py:164
  160.4 6.4 %all-to-all-start.1 = ((f32[8,3,64,128]{3,2,1,0:T(8,128)}), f32[8,3,64,128]{3,2,1,0:T(8,128)S(1)}, u32[]{:S(2)}, u32[]{:S(2)}) async-start(f32[8,3,64,128]{3,2,1,0:T(8,128)} %copy.46), calls=%async_computation.1 | async-start | bytes 1572864 | tf_op jit(solution)/shard_map/all_to_all | solution.py:194
  168.0 2.1 collective-permute-start
  170.1 1.5 collective-permute-start.1
  172.3 2.9 %collective-permute-start.3 = (f32[1,3,64]{2,0,1:T(1,128)S(1)}, f32[1,3,64]{2,0,1:T(1,128)S(1)}, u32[]{:S(2)}, u32[]{:S(2)}) collective-permute-start(f32[1,3,64]{2,0,1:T(1,128)S(1)} %get-tuple-element.442), channel_id=1, source_target_pairs={{0,16},{4,20},{8,24},{12,28},{16,0},{20,4},{24,8},{28,12},{1,17},{... | collective-permute-start | bytes 2312 | tf_op jit(solution)/shard_map/ppermute | solution.py:20
  175.2 1.5 collective-permute-start.4
  176.7 3.3 %collective-permute-start.5 = (f32[1,3,64]{2,0,1:T(1,128)S(1)}, f32[1,3,64]{2,0,1:T(1,128)S(1)}, u32[]{:S(2)}, u32[]{:S(2)}) collective-permute-start(f32[1,3,64]{2,0,1:T(1,128)S(1)} %get-tuple-element.440), channel_id=1, source_target_pairs={{0,24},{4,28},{8,16},{12,20},{16,8},{20,12},{24,0},{28,4},{1,25},{... | collective-permute-start | bytes 2312 | tf_op jit(solution)/shard_map/ppermute | solution.py:20
  179.9 4.2 %collective-permute-start.6 = (f32[1,3,64]{2,0,1:T(1,128)S(1)}, f32[1,3,64]{2,0,1:T(1,128)S(1)}, u32[]{:S(2)}, u32[]{:S(2)}) collective-permute-start(f32[1,3,64]{2,0,1:T(1,128)S(1)} %get-tuple-element.439), channel_id=1, source_target_pairs={{0,28},{4,24},{8,20},{12,16},{16,12},{20,8},{24,4},{28,0},{1,29},{... | collective-permute-start | bytes 2312 | tf_op jit(solution)/shard_map/ppermute | solution.py:20
  184.4 2.7 %collective-permute-done.3 = f32[1,3,64]{2,0,1:T(1,128)S(1)} collective-permute-done((f32[1,3,64]{2,0,1:T(1,128)S(1)}, f32[1,3,64]{2,0,1:T(1,128)S(1)}, u32[]{:S(2)}, u32[]{:S(2)}) %collective-permute-start.3) | collective-permute-done | bytes 800 | tf_op jit(solution)/shard_map/ppermute | solution.py:20
  187.1 0.7 collective-permute-done.4
  188.0 1.5 fusion.158
  189.5 0.7 reshape.681
  190.2 1.2 bitcast_divide_fusion
  191.4 0.8 fusion.78
  192.2 20.2 %pmax.7 = f32[1]{0:T(128)} all-reduce(f32[1]{0:T(128)} %bitcast.60), channel_id=1, replica_groups=mesh['tile'=8,'cplx'=4] {'tile'}, use_global_device_ids=true, to_apply=%region_32.33 | all-reduce | flops 1 | bytes 8 | tf_op jit(solution)/shard_map/pmax | solution.py:220
  (172 shorter events, 26.3 us)
Async XLA Ops:
  6.1 9.0 %copy-start.3 = (s32[4]{0:T(128)S(1)}, s32[4]{0:T(128)}, u32[]{:S(2)}) copy-start(s32[4]{0:T(128)} %param.17) | copy-start | bytes 52
  6.1 10.3 %copy-start = (bf16[128,64]{0,1:T(8,128)(2,1)S(1)}, bf16[128,64]{0,1:T(8,128)(2,1)}, u32[]{:S(2)}) copy-start(bf16[128,64]{0,1:T(8,128)(2,1)} %param.22) | copy-start | bytes 49156
  6.2 10.3 %copy-start.1 = (f32[64]{0:T(128)S(1)}, f32[64]{0:T(128)}, u32[]{:S(2)}) copy-start(f32[64]{0:T(128)} %param.23) | copy-start | bytes 772
  6.2 10.3 %copy-start.4 = (bf16[128,512]{1,0:T(8,128)(2,1)S(1)}, bf16[128,512]{1,0:T(8,128)(2,1)}, u32[]{:S(2)}) copy-start(bf16[128,512]{1,0:T(8,128)(2,1)} %param.20) | copy-start | bytes 393220
  6.2 10.3 %copy-start.5 = (bf16[512,128]{1,0:T(8,128)(2,1)S(1)}, bf16[512,128]{1,0:T(8,128)(2,1)}, u32[]{:S(2)}) copy-start(bf16[512,128]{1,0:T(8,128)(2,1)} %param.21) | copy-start | bytes 393220
  6.2 10.3 %copy-start.6 = (f32[128]{0:T(128)S(1)}, f32[128]{0:T(128)}, u32[]{:S(2)}) copy-start(f32[128]{0:T(128)} %param.19) | copy-start | bytes 1540
  16.5 38.8 %copy-start.2 = (s32[4,512]{1,0:T(4,128)S(1)}, s32[4,512]{1,0:T(4,128)}, u32[]{:S(2)}) copy-start(s32[4,512]{1,0:T(4,128)} %param.18) | copy-start | bytes 24580
  140.8 10.2 %all-to-all-start = ((f32[4,128,128]{2,1,0:T(8,128)}), f32[4,128,128]{2,1,0:T(8,128)S(1)}, u32[]{:S(2)}, u32[]{:S(2)}) async-start(f32[4,128,128]{2,1,0:T(8,128)} %copy.41), calls=%async_computation | async-start | bytes 524288 | tf_op jit(solution)/shard_map/all_to_all | solution.py:163
  151.1 9.4 %all-to-all-start.2 = ((f32[4,128,128]{2,1,0:T(8,128)}), f32[4,128,128]{2,1,0:T(8,128)S(1)}, u32[]{:S(2)}, u32[]{:S(2)}) async-start(f32[4,128,128]{2,1,0:T(8,128)} %copy.51), calls=%async_computation.2 | async-start | bytes 524288 | tf_op jit(solution)/shard_map/all_to_all | solution.py:164
  160.4 27.5 %all-to-all-start.1 = ((f32[8,3,64,128]{3,2,1,0:T(8,128)}), f32[8,3,64,128]{3,2,1,0:T(8,128)S(1)}, u32[]{:S(2)}, u32[]{:S(2)}) async-start(f32[8,3,64,128]{3,2,1,0:T(8,128)} %copy.46), calls=%async_computation.1 | async-start | bytes 1572864 | tf_op jit(solution)/shard_map/all_to_all | solution.py:194
  168.0 8.7 %collective-permute-start = (f32[1,3,64]{2,0,1:T(1,128)S(1)}, f32[1,3,64]{2,0,1:T(1,128)S(1)}, u32[]{:S(2)}, u32[]{:S(2)}) collective-permute-start(f32[1,3,64]{2,0,1:T(1,128)S(1)} %get-tuple-element.445), channel_id=1, source_target_pairs={{0,4},{4,0},{8,12},{12,8},{16,20},{20,16},{24,28},{28,24},{1,5},{5... | collective-permute-start | bytes 2312 | tf_op jit(solution)/shard_map/ppermute | solution.py:20
  170.1 9.8 %collective-permute-start.1 = (f32[1,3,64]{2,0,1:T(1,128)S(1)}, f32[1,3,64]{2,0,1:T(1,128)S(1)}, u32[]{:S(2)}, u32[]{:S(2)}) collective-permute-start(f32[1,3,64]{2,0,1:T(1,128)S(1)} %get-tuple-element.444), channel_id=1, source_target_pairs={{0,8},{4,12},{8,0},{12,4},{16,24},{20,28},{24,16},{28,20},{1,9},{5... | collective-permute-start | bytes 2312 | tf_op jit(solution)/shard_map/ppermute | solution.py:20
  172.3 12.0 %collective-permute-start.2 = (f32[1,3,64]{2,0,1:T(1,128)S(1)}, f32[1,3,64]{2,0,1:T(1,128)S(1)}, u32[]{:S(2)}, u32[]{:S(2)}) collective-permute-start(f32[1,3,64]{2,0,1:T(1,128)S(1)} %get-tuple-element.443), channel_id=1, source_target_pairs={{0,12},{4,8},{8,4},{12,0},{16,28},{20,24},{24,20},{28,16},{1,13},{... | collective-permute-start | bytes 2312 | tf_op jit(solution)/shard_map/ppermute | solution.py:20
  172.3 14.8 %collective-permute-start.3 = (f32[1,3,64]{2,0,1:T(1,128)S(1)}, f32[1,3,64]{2,0,1:T(1,128)S(1)}, u32[]{:S(2)}, u32[]{:S(2)}) collective-permute-start(f32[1,3,64]{2,0,1:T(1,128)S(1)} %get-tuple-element.442), channel_id=1, source_target_pairs={{0,16},{4,20},{8,24},{12,28},{16,0},{20,4},{24,8},{28,12},{1,17},{... | collective-permute-start | bytes 2312 | tf_op jit(solution)/shard_map/ppermute | solution.py:20
  175.2 12.6 %collective-permute-start.4 = (f32[1,3,64]{2,0,1:T(1,128)S(1)}, f32[1,3,64]{2,0,1:T(1,128)S(1)}, u32[]{:S(2)}, u32[]{:S(2)}) collective-permute-start(f32[1,3,64]{2,0,1:T(1,128)S(1)} %get-tuple-element.441), channel_id=1, source_target_pairs={{0,20},{4,16},{8,28},{12,24},{16,4},{20,0},{24,12},{28,8},{1,21},{... | collective-permute-start | bytes 2312 | tf_op jit(solution)/shard_map/ppermute | solution.py:20
  176.7 11.2 %collective-permute-start.5 = (f32[1,3,64]{2,0,1:T(1,128)S(1)}, f32[1,3,64]{2,0,1:T(1,128)S(1)}, u32[]{:S(2)}, u32[]{:S(2)}) collective-permute-start(f32[1,3,64]{2,0,1:T(1,128)S(1)} %get-tuple-element.440), channel_id=1, source_target_pairs={{0,24},{4,28},{8,16},{12,20},{16,8},{20,12},{24,0},{28,4},{1,25},{... | collective-permute-start | bytes 2312 | tf_op jit(solution)/shard_map/ppermute | solution.py:20
  179.9 8.0 %collective-permute-start.6 = (f32[1,3,64]{2,0,1:T(1,128)S(1)}, f32[1,3,64]{2,0,1:T(1,128)S(1)}, u32[]{:S(2)}, u32[]{:S(2)}) collective-permute-start(f32[1,3,64]{2,0,1:T(1,128)S(1)} %get-tuple-element.439), channel_id=1, source_target_pairs={{0,28},{4,24},{8,20},{12,16},{16,12},{20,8},{24,4},{28,0},{1,29},{... | collective-permute-start | bytes 2312 | tf_op jit(solution)/shard_map/ppermute | solution.py:20
